TPU v7x, 512 devices: a whole 4x8x8 slice. The times are simulated.
512 devices in a mesh: win: 128 (over y, z, core), head: 4 (over x).
Axes of the slice: x: 4, y: 8, z: 8, core: 2. Of those that a mesh axis runs over, the one named last changes fastest.
Arguments:
- tokens: bfloat16 [16384, 2560], P('win', 'head'), may hold values from -6 to 6
- queries: bfloat16 [16384, 1536], P('win', 'head'), may hold values from -64 to 64, as said below
- key_weight: bfloat16 [2560, 1536], P(None, 'head'), may hold values from -0.125 to 0.125
- value_weight: bfloat16 [2560, 1536], P(None, 'head'), may hold values from -0.125 to 0.125
- grad_out: bfloat16 [16384, 1536], P('win', 'head'), may hold values from -6 to 6
- owner_table: int32 [128, 64], replicated, may hold values from 0 to 127, as said below
- window_table: int32 [128, 64], replicated, may hold values from 0 to 16511, as said below
Outputs:
- attended: bfloat16 [16384, 1536], P('win', 'head')
- grad_queries: bfloat16 [16384, 1536], P('win', 'head')
- grad_tokens: bfloat16 [16384, 2560], P('win', 'head')
Inputs may be any that keep to these rules, and one draw needn't show every extreme that they name: `owner_table`: the 64 groups of one window group go to distinct owners; in every draw some owner receives a group from every window group. `window_table`: groups with the same window number have the same owner. `queries`: rows may have scales far from one.
All inputs are finite; a program needn't handle non-finite values.
Results may differ from a plain program's by a relative error of at most 0.025.
The roundings to bfloat16 on the way count: a program that leaves them out, or rounds other values in their place, can miss the bound.
Values may be sent and summed in bfloat16 or wider, within the bound.
No kernel may reach another device: no remote copies, remote signals or barrier semaphores. Data moves between devices by JAX's collectives and lax.ppermute only.
A program may use at most 64 MiB of HBM per device.

v0:
```python
import math

import jax
import jax.numpy as jnp
from jax import lax
from jax.sharding import PartitionSpec as P

HD = 128


def attend_forward(q_slots, k_slots, v_slots, same_window):
    devices, group_rows, width = q_slots.shape
    slot_count = devices * group_rows
    head_count = width // HD
    scale = 1.0 / math.sqrt(HD)
    query = q_slots.reshape(slot_count, head_count, HD)
    key = k_slots.reshape(slot_count, head_count, HD)
    value = v_slots.reshape(slot_count, head_count, HD)
    scores = jnp.einsum("qhd,khd->hqk", query, key, preferred_element_type=jnp.float32) * scale
    scores = jnp.where(same_window[None], scores, -1e30)
    top = jnp.max(scores, axis=-1, keepdims=True)
    expd = jnp.exp(scores - top)
    weights = expd / jnp.sum(expd, axis=-1, keepdims=True)
    weights_low = weights.astype(jnp.bfloat16)
    output = jnp.einsum(
        "hqk,khd->qhd", weights_low, value, preferred_element_type=jnp.float32
    ).astype(jnp.bfloat16)
    return (weights, output.reshape(devices, group_rows, width))


def attend_backward(weights, q_slots, k_slots, v_slots, o_slots, do_slots):
    devices, group_rows, width = q_slots.shape
    slot_count = devices * group_rows
    head_count = width // HD
    scale = 1.0 / math.sqrt(HD)
    query = q_slots.reshape(slot_count, head_count, HD)
    key = k_slots.reshape(slot_count, head_count, HD)
    value = v_slots.reshape(slot_count, head_count, HD)
    output = o_slots.reshape(slot_count, head_count, HD)
    dout = do_slots.reshape(slot_count, head_count, HD)
    weights_low = weights.astype(jnp.bfloat16)
    grad_v = jnp.einsum("hqk,qhd->khd", weights_low, dout, preferred_element_type=jnp.float32)
    grad_p = jnp.einsum("qhd,khd->hqk", dout, value, preferred_element_type=jnp.float32)
    delta = jnp.einsum("qhd,qhd->hq", dout, output, preferred_element_type=jnp.float32)
    grad_s_low = (weights * (grad_p - delta[:, :, None])).astype(jnp.bfloat16)
    grad_q = jnp.einsum("hqk,khd->qhd", grad_s_low, key, preferred_element_type=jnp.float32) * scale
    grad_k = (
        jnp.einsum("hqk,qhd->khd", grad_s_low, query, preferred_element_type=jnp.float32) * scale
    )
    shape = (devices, group_rows, width)
    return (
        grad_q.astype(jnp.bfloat16).reshape(shape),
        grad_k.astype(jnp.bfloat16).reshape(shape),
        grad_v.astype(jnp.bfloat16).reshape(shape),
    )


def local(tokens, queries, key_weight, value_weight, grad_out, owner_table, window_table):
    devices = lax.axis_size("win")
    own_index = lax.axis_index("win")
    pick_count = owner_table.shape[1]
    tok_rows = tokens.shape[0]
    group_rows = tok_rows // pick_count
    owners = jnp.arange(devices, dtype=jnp.int32)
    own_owners = lax.dynamic_index_in_dim(owner_table, own_index, 0, keepdims=False)
    send_select = (own_owners[None, :] == owners[:, None]).astype(jnp.bfloat16)

    def to_slots(rows):
        columns = rows.shape[1]
        packed = jnp.dot(
            send_select,
            rows.reshape(pick_count, group_rows * columns),
            preferred_element_type=jnp.float32,
        )
        return packed.astype(jnp.bfloat16).reshape(devices, group_rows, columns)

    def from_slots(slot_rows):
        columns = slot_rows.shape[2]
        flat = slot_rows.reshape(devices, group_rows * columns)
        picked = lax.dot_general(
            send_select, flat, (((0,), (0,)), ((), ())), preferred_element_type=jnp.float32
        )
        return picked.astype(jnp.bfloat16).reshape(tok_rows, columns)

    sent_here = owner_table == own_index
    filled = jnp.any(sent_here, axis=1)
    slot_windows = jnp.sum(jnp.where(sent_here, window_table, 0), axis=1)
    slot_windows = jnp.where(filled, slot_windows, -(owners + 1))
    token_windows = jnp.repeat(slot_windows, group_rows)
    same_window = token_windows[:, None] == token_windows[None, :]
    piece = lax.all_gather(tokens, "head", axis=1, tiled=True)
    columns = piece.shape[1]
    key_sum = jnp.dot(piece, key_weight, preferred_element_type=jnp.float32)
    value_sum = jnp.dot(piece, value_weight, preferred_element_type=jnp.float32)
    key_low = key_sum.astype(jnp.bfloat16)
    value_low = value_sum.astype(jnp.bfloat16)
    q_slots, k_slots, v_slots = (
        lax.all_to_all(to_slots(queries), "win", split_axis=0, concat_axis=0, tiled=True),
        lax.all_to_all(to_slots(key_low), "win", split_axis=0, concat_axis=0, tiled=True),
        lax.all_to_all(to_slots(value_low), "win", split_axis=0, concat_axis=0, tiled=True),
    )
    weights, o_slots = attend_forward(q_slots, k_slots, v_slots, same_window)
    o_back = lax.all_to_all(o_slots, "win", split_axis=0, concat_axis=0, tiled=True)
    do_slots = lax.all_to_all(to_slots(grad_out), "win", split_axis=0, concat_axis=0, tiled=True)
    grad_q_slots, grad_k_slots, grad_v_slots = attend_backward(
        weights, q_slots, k_slots, v_slots, o_slots, do_slots
    )
    dq_back, dk_back, dv_back = (
        lax.all_to_all(grad_q_slots, "win", split_axis=0, concat_axis=0, tiled=True),
        lax.all_to_all(grad_k_slots, "win", split_axis=0, concat_axis=0, tiled=True),
        lax.all_to_all(grad_v_slots, "win", split_axis=0, concat_axis=0, tiled=True),
    )
    grad_queries = from_slots(dq_back)
    contract = (((1,), (1,)), ((), ()))
    term = lax.dot_general(
        from_slots(dk_back), key_weight, contract, preferred_element_type=jnp.float32
    )
    term = term + lax.dot_general(
        from_slots(dv_back), value_weight, contract, preferred_element_type=jnp.float32
    )
    grad_tokens = lax.psum_scatter(term, "head", scatter_dimension=1, tiled=True).astype(
        jnp.bfloat16
    )
    attended = from_slots(o_back)
    return (attended, grad_queries, grad_tokens)


def solution(mesh):
    in_specs = (
        P("win", "head"),
        P("win", "head"),
        P(None, "head"),
        P(None, "head"),
        P("win", "head"),
        P(),
        P(),
    )
    out_specs = (P("win", "head"), P("win", "head"), P("win", "head"))
    return jax.shard_map(local, mesh=mesh, in_specs=in_specs, out_specs=out_specs, check_vma=False)
```

profile of v0, /device:TPU:2, one launch (start us, length us, event | category | flops | bytes accessed | tf_op | source)
XLA Modules:
  0.0 212.9 jit_solution(6095350091950178469)
XLA Ops:
  7.2 1.1 reshape.120
  8.3 0.9 dynamic-slice_reduce_fusion
  9.2 0.2 convolution_convert_fusion.2
  9.4 0.7 reshape.121
  10.2 17.8 %all-to-all-start.1 = ((bf16[128,2,384]{2,1,0:T(2,128)(2,1)}), bf16[128,2,384]{2,1,0:T(2,128)(2,1)S(1)}, u32[]{:S(2)}, u32[]{:S(2)}) async-start(bf16[128,2,384]{2,1,0:T(2,128)(2,1)} %reshape.121), calls=%async_computation.1 | async-start | bytes 393216 | tf_op jit(solution)/shard_map/all_to_all | solution.py:98
  28.0 0.8 select_reduce_fusion
  28.8 0.9 reshape.129
  29.7 0.2 convolution_convert_fusion
  29.9 14.2 %all_gather.3 = bf16[128,2560]{1,0:T(8,128)(2,1)S(1)} all-gather(bf16[128,640]{1,0:T(8,128)(2,1)S(1)} %copy-done.6), channel_id=1, replica_groups=mesh['win'=128,'head'=4] {'head'}, dimensions={1}, use_global_device_ids=true | all-gather | bytes 819200 | tf_op jit(solution)/shard_map/all_gather | solution.py:91
  44.2 0.1 eq.46
  44.4 0.7 reshape.130
  45.1 2.1 convolution_convert_fusion.7
  47.2 13.8 %all-to-all-start.4 = ((bf16[128,2,384]{2,1,0:T(2,128)(2,1)}), bf16[128,2,384]{2,1,0:T(2,128)(2,1)S(1)}, u32[]{:S(2)}, u32[]{:S(2)}) async-start(bf16[128,2,384]{2,1,0:T(2,128)(2,1)} %reshape.130), calls=%async_computation.4 | async-start | bytes 393216 | tf_op jit(solution)/shard_map/all_to_all | solution.py:104
  61.1 0.5 convolution_convert_fusion.6
  61.6 0.2 convolution_convert_fusion.1
  61.8 0.7 reshape.124
  62.6 12.2 %all-to-all-done.4 = bf16[128,2,384]{2,1,0:T(2,128)(2,1)S(1)} async-done(((bf16[128,2,384]{2,1,0:T(2,128)(2,1)}), bf16[128,2,384]{2,1,0:T(2,128)(2,1)S(1)}, u32[]{:S(2)}, u32[]{:S(2)}) %all-to-all-start.4) | async-done | bytes 196640 | tf_op jit(solution)/shard_map/all_to_all | solution.py:104
  74.8 6.2 %all-to-all-start.2 = ((bf16[128,2,384]{2,1,0:T(2,128)(2,1)}), bf16[128,2,384]{2,1,0:T(2,128)(2,1)S(1)}, u32[]{:S(2)}, u32[]{:S(2)}) async-start(bf16[128,2,384]{2,1,0:T(2,128)(2,1)} %reshape.124), calls=%async_computation.2 | async-start | bytes 393216 | tf_op jit(solution)/shard_map/all_to_all | solution.py:99
  80.9 0.2 convolution_convert_fusion.3
  81.1 0.7 reshape.118
  82.0 0.1 reshape.122
  82.1 0.2 copy.33
  82.4 0.8 copy.37
  83.3 11.4 %all-to-all-done.2 = bf16[128,2,384]{2,1,0:T(2,128)(2,1)S(1)} async-done(((bf16[128,2,384]{2,1,0:T(2,128)(2,1)}), bf16[128,2,384]{2,1,0:T(2,128)(2,1)S(1)}, u32[]{:S(2)}, u32[]{:S(2)}) %all-to-all-start.2) | async-done | bytes 196640 | tf_op jit(solution)/shard_map/all_to_all | solution.py:99
  94.7 6.3 %all-to-all-start = ((bf16[128,2,384]{2,1,0:T(2,128)(2,1)}), bf16[128,2,384]{2,1,0:T(2,128)(2,1)S(1)}, u32[]{:S(2)}, u32[]{:S(2)}) async-start(bf16[128,2,384]{2,1,0:T(2,128)(2,1)} %reshape.118), calls=%async_computation | async-start | bytes 393216 | tf_op jit(solution)/shard_map/all_to_all | solution.py:100
  101.1 0.9 copy.48
  102.2 0.2 copy.29
  102.3 1.3 fusion.32
  103.7 10.9 %all-to-all-done = bf16[128,2,384]{2,1,0:T(2,128)(2,1)S(1)} async-done(((bf16[128,2,384]{2,1,0:T(2,128)(2,1)}), bf16[128,2,384]{2,1,0:T(2,128)(2,1)S(1)}, u32[]{:S(2)}, u32[]{:S(2)}) %all-to-all-start) | async-done | bytes 196640 | tf_op jit(solution)/shard_map/all_to_all | solution.py:100
  114.7 1.3 multiply_reduce_fusion
  116.1 1.5 fusion.5
  117.5 0.3 fusion.8
  117.8 0.2 copy.35
  118.0 0.8 reshape.135
  118.8 6.2 %all-to-all-start.6 = ((bf16[128,2,384]{2,1,0:T(2,128)(2,1)}), bf16[128,2,384]{2,1,0:T(2,128)(2,1)S(1)}, u32[]{:S(2)}, u32[]{:S(2)}) async-start(bf16[128,2,384]{2,1,0:T(2,128)(2,1)} %reshape.135), calls=%async_computation.6 | async-start | bytes 393216 | tf_op jit(solution)/shard_map/all_to_all | solution.py:110
  125.0 2.3 %fusion.10 = bf16[256,3,128]{0,2,1:T(8,128)(2,1)} fusion(bf16[256,3,128]{0,2,1:T(8,128)(2,1)} %copy.37, f32[3,256]{1,0:T(4,128)S(1)} %get-tuple-element.5, bf16[256,3,128]{0,2,1:T(8,128)(2,1)S(1)} %copy.33, bf16[256,3,128]{0,2,1:T(8,128)(2,1)S(1)} %copy.29, pred[256,256]{0,1:T(8,128)(4,1)S(1)} %broadcast_compare_fusion), kind=kOutput, calls=%fused_computation.21 | convolution fusion | flops 101745664 | bytes 855040 | tf_op jit(solution)/shard_map/hqk,qhd->khd/dot_general | solution.py:42
  127.3 1.1 copy.39
  128.4 0.9 reshape.138
  129.3 9.5 %all-to-all-done.6 = bf16[128,2,384]{2,1,0:T(2,128)(2,1)S(1)} async-done(((bf16[128,2,384]{2,1,0:T(2,128)(2,1)}), bf16[128,2,384]{2,1,0:T(2,128)(2,1)S(1)}, u32[]{:S(2)}, u32[]{:S(2)}) %all-to-all-start.6) | async-done | bytes 196640 | tf_op jit(solution)/shard_map/all_to_all | solution.py:110
  138.7 6.1 %all-to-all-start.7 = ((bf16[128,2,384]{2,1,0:T(2,128)(2,1)}), bf16[128,2,384]{2,1,0:T(2,128)(2,1)S(1)}, u32[]{:S(2)}, u32[]{:S(2)}) async-start(bf16[128,2,384]{2,1,0:T(2,128)(2,1)} %reshape.138), calls=%async_computation.7 | async-start | bytes 393216 | tf_op jit(solution)/shard_map/all_to_all | solution.py:111
  144.9 0.2 copy.36
  145.1 0.2 convolution_convert_fusion.9
  145.4 13.2 %all-to-all-done.7 = bf16[128,2,384]{2,1,0:T(2,128)(2,1)S(1)} async-done(((bf16[128,2,384]{2,1,0:T(2,128)(2,1)}), bf16[128,2,384]{2,1,0:T(2,128)(2,1)S(1)}, u32[]{:S(2)}, u32[]{:S(2)}) %all-to-all-start.7) | async-done | bytes 196640 | tf_op jit(solution)/shard_map/all_to_all | solution.py:111
  158.6 0.2 copy.40
  158.8 0.2 convolution_convert_fusion.8
  159.1 0.7 fusion.33
  159.8 0.8 copy-done.1
  160.6 1.8 convolution_add_fusion
  162.5 0.2 copy.24
  162.7 0.9 reshape.126
  163.5 6.2 %all-to-all-start.3 = ((bf16[128,2,384]{2,1,0:T(2,128)(2,1)}), bf16[128,2,384]{2,1,0:T(2,128)(2,1)S(1)}, u32[]{:S(2)}, u32[]{:S(2)}) async-start(bf16[128,2,384]{2,1,0:T(2,128)(2,1)} %reshape.126), calls=%async_computation.3 | async-start | bytes 393216 | tf_op jit(solution)/shard_map/all_to_all | solution.py:103
  169.7 0.2 fusion.9
  169.9 0.2 copy.31
  170.1 0.9 reshape.132
  171.0 12.5 %all-to-all-done.3 = bf16[128,2,384]{2,1,0:T(2,128)(2,1)S(1)} async-done(((bf16[128,2,384]{2,1,0:T(2,128)(2,1)}), bf16[128,2,384]{2,1,0:T(2,128)(2,1)S(1)}, u32[]{:S(2)}, u32[]{:S(2)}) %all-to-all-start.3) | async-done | bytes 196640 | tf_op jit(solution)/shard_map/all_to_all | solution.py:103
  183.4 6.1 %all-to-all-start.5 = ((bf16[128,2,384]{2,1,0:T(2,128)(2,1)}), bf16[128,2,384]{2,1,0:T(2,128)(2,1)S(1)}, u32[]{:S(2)}, u32[]{:S(2)}) async-start(bf16[128,2,384]{2,1,0:T(2,128)(2,1)} %reshape.132), calls=%async_computation.5 | async-start | bytes 393216 | tf_op jit(solution)/shard_map/all_to_all | solution.py:109
  189.6 0.2 copy.25
  189.8 0.2 convolution_convert_fusion.11
  190.0 0.7 reshape.128
  190.7 12.6 %all-to-all-done.5 = bf16[128,2,384]{2,1,0:T(2,128)(2,1)S(1)} async-done(((bf16[128,2,384]{2,1,0:T(2,128)(2,1)}), bf16[128,2,384]{2,1,0:T(2,128)(2,1)S(1)}, u32[]{:S(2)}, u32[]{:S(2)}) %all-to-all-start.5) | async-done | bytes 196640 | tf_op jit(solution)/shard_map/all_to_all | solution.py:109
  203.3 0.2 copy.32
  203.5 0.2 convolution_convert_fusion.10
  203.7 0.7 reshape.134
  204.4 1.7 convert_element_type.85
  (29 shorter events, 0.9 us)
Async XLA Ops:
  7.2 53.9 %copy-start = (bf16[2560,384]{1,0:T(8,128)(2,1)S(1)}, bf16[2560,384]{1,0:T(8,128)(2,1)}, u32[]{:S(2)}) copy-start(bf16[2560,384]{1,0:T(8,128)(2,1)} %param.9) | copy-start | bytes 5898244
  7.2 22.7 %copy-start.6 = (bf16[128,640]{1,0:T(8,128)(2,1)S(1)}, bf16[128,640]{1,0:T(8,128)(2,1)}, u32[]{:S(2)}) copy-start(bf16[128,640]{1,0:T(8,128)(2,1)} %param.7) | copy-start | bytes 491524
  10.2 37.1 %all-to-all-start.1 = ((bf16[128,2,384]{2,1,0:T(2,128)(2,1)}), bf16[128,2,384]{2,1,0:T(2,128)(2,1)S(1)}, u32[]{:S(2)}, u32[]{:S(2)}) async-start(bf16[128,2,384]{2,1,0:T(2,128)(2,1)} %reshape.121), calls=%async_computation.1 | async-start | bytes 393216 | tf_op jit(solution)/shard_map/all_to_all | solution.py:98
  47.2 27.5 %all-to-all-start.4 = ((bf16[128,2,384]{2,1,0:T(2,128)(2,1)}), bf16[128,2,384]{2,1,0:T(2,128)(2,1)S(1)}, u32[]{:S(2)}, u32[]{:S(2)}) async-start(bf16[128,2,384]{2,1,0:T(2,128)(2,1)} %reshape.130), calls=%async_computation.4 | async-start | bytes 393216 | tf_op jit(solution)/shard_map/all_to_all | solution.py:104
  74.8 19.9 %all-to-all-start.2 = ((bf16[128,2,384]{2,1,0:T(2,128)(2,1)}), bf16[128,2,384]{2,1,0:T(2,128)(2,1)S(1)}, u32[]{:S(2)}, u32[]{:S(2)}) async-start(bf16[128,2,384]{2,1,0:T(2,128)(2,1)} %reshape.124), calls=%async_computation.2 | async-start | bytes 393216 | tf_op jit(solution)/shard_map/all_to_all | solution.py:99
  94.7 19.9 %all-to-all-start = ((bf16[128,2,384]{2,1,0:T(2,128)(2,1)}), bf16[128,2,384]{2,1,0:T(2,128)(2,1)S(1)}, u32[]{:S(2)}, u32[]{:S(2)}) async-start(bf16[128,2,384]{2,1,0:T(2,128)(2,1)} %reshape.118), calls=%async_computation | async-start | bytes 393216 | tf_op jit(solution)/shard_map/all_to_all | solution.py:100
  102.0 12.7 %copy-start.2 = (f32[3,256,128]{1,2,0:T(8,128)S(1)}, f32[3,256,128]{1,2,0:T(8,128)}, u32[]{:S(2)}) copy-start(f32[3,256,128]{1,2,0:T(8,128)} %copy.48) | copy-start | bytes 1179652
  114.7 1.3 copy-start.3
  114.7 1.3 copy-start.5
  118.8 19.9 %all-to-all-start.6 = ((bf16[128,2,384]{2,1,0:T(2,128)(2,1)}), bf16[128,2,384]{2,1,0:T(2,128)(2,1)S(1)}, u32[]{:S(2)}, u32[]{:S(2)}) async-start(bf16[128,2,384]{2,1,0:T(2,128)(2,1)} %reshape.135), calls=%async_computation.6 | async-start | bytes 393216 | tf_op jit(solution)/shard_map/all_to_all | solution.py:110
  138.7 19.9 %all-to-all-start.7 = ((bf16[128,2,384]{2,1,0:T(2,128)(2,1)}), bf16[128,2,384]{2,1,0:T(2,128)(2,1)S(1)}, u32[]{:S(2)}, u32[]{:S(2)}) async-start(bf16[128,2,384]{2,1,0:T(2,128)(2,1)} %reshape.138), calls=%async_computation.7 | async-start | bytes 393216 | tf_op jit(solution)/shard_map/all_to_all | solution.py:111
  144.9 59.6 %reduce-scatter.2.cloned.1.call-start = ((), (), s32[]{:S(2)}) async-start(), calls=%async_computation.9 | async-start | bytes 1638400 | tf_op jit(solution)/shard_map/reduce_scatter | solution.py:121
  159.1 1.5 copy-start.1
  160.6 1.8 copy-start.4
  163.5 19.9 %all-to-all-start.3 = ((bf16[128,2,384]{2,1,0:T(2,128)(2,1)}), bf16[128,2,384]{2,1,0:T(2,128)(2,1)S(1)}, u32[]{:S(2)}, u32[]{:S(2)}) async-start(bf16[128,2,384]{2,1,0:T(2,128)(2,1)} %reshape.126), calls=%async_computation.3 | async-start | bytes 393216 | tf_op jit(solution)/shard_map/all_to_all | solution.py:103
  183.4 19.9 %all-to-all-start.5 = ((bf16[128,2,384]{2,1,0:T(2,128)(2,1)}), bf16[128,2,384]{2,1,0:T(2,128)(2,1)S(1)}, u32[]{:S(2)}, u32[]{:S(2)}) async-start(bf16[128,2,384]{2,1,0:T(2,128)(2,1)} %reshape.132), calls=%async_computation.5 | async-start | bytes 393216 | tf_op jit(solution)/shard_map/all_to_all | solution.py:109
Sparse Core Ops, SparseCore 0:
  162.6 19.8 reduce-scatter.1
where the time goes:
time: 214 us; the launch traced here: 213 us
  waiting for transfers between devices  82.2 us (38%)
  starting transfers between devices  68.8 us (32%)
  local copies, waits for them, and re-layouts  17.1 us (8%)
  between operations  14.4 us (7%)
  blocking collectives  14.2 us (7%)
  matrix products  13.6 us (6%)
  other arithmetic  2.66 us (1%)
    all_to_all x1, starting transfers between devices, local(): lax.all_to_all(to_slots(queries), 'win', split_axis=0, concat_axis=0, til...  17.8 us
    all_gather x1, blocking collectives, local(): piece = lax.all_gather(tokens, 'head', axis=1, tiled=True)  14.2 us
    all_to_all x1, starting transfers between devices, local(): lax.all_to_all(to_slots(grad_out), 'win', split_axis=0, concat_axis=0, ti...  13.8 us
    all_to_all x1, waiting for transfers between devices, local(): lax.all_to_all(grad_v_slots, 'win', split_axis=0, concat_axis=0, tiled=True)  13.2 us
    all_to_all x1, waiting for transfers between devices, local(): lax.all_to_all(grad_q_slots, 'win', split_axis=0, concat_axis=0, tiled=True)  12.6 us
    all_to_all x1, waiting for transfers between devices, local(): lax.all_to_all(o_slots, 'win', split_axis=0, concat_axis=0, tiled=True)  12.5 us
    all_to_all x1, waiting for transfers between devices, local(): lax.all_to_all(to_slots(grad_out), 'win', split_axis=0, concat_axis=0, ti...  12.2 us
    all_to_all x1, waiting for transfers between devices, local(): lax.all_to_all(to_slots(key_low), 'win', split_axis=0, concat_axis=0, til...  11.4 us
  transfers between devices with their start and end apart: 9, of which 7 were waited for; matrix products, arithmetic and copies ran while one was open for 10% of the time, Pallas kernels for 0%

commit v1 on v0

v1 whole, which is shorter than its diff:
```python
import math

import jax
import jax.numpy as jnp
from jax import lax
from jax.experimental import pallas as pl
from jax.experimental.pallas import tpu as pltpu
from jax.sharding import PartitionSpec as P

HD = 128
KINDS = 4
F32 = jnp.float32
BF16 = jnp.bfloat16
NN = (((1,), (0,)), ((), ()))
NT = (((1,), (1,)), ((), ()))
TN = (((0,), (0,)), ((), ()))


def dot(a, b, dims=NN):
    return lax.dot_general(a, b, dims, preferred_element_type=F32)


def iota(shape, dim):
    return lax.broadcasted_iota(jnp.int32, shape, dim)


def own_owners(owner_ref, group_rows, along):
    picks = owner_ref.shape[1]
    own = owner_ref[pl.ds(lax.axis_index("win"), 1), :]
    own = jnp.broadcast_to(own.astype(F32), (8, picks)).astype(BF16)
    tok = picks * group_rows
    if along == 1:
        spread = iota((picks, tok), 1) // group_rows == iota((picks, tok), 0)
        return dot(own, spread.astype(F32).astype(BF16))[0:1, :].astype(jnp.int32)
    spread = iota((tok, picks), 0) // group_rows == iota((tok, picks), 1)
    return dot(spread.astype(F32).astype(BF16), own, NT)[:, 0:1].astype(jnp.int32)


def targets(owner_ref, group_rows, along):
    own = own_owners(owner_ref, group_rows, along)
    inner = iota(own.shape, along) % group_rows
    parts = [own * (KINDS * group_rows) + kind * group_rows + inner for kind in range(KINDS)]
    return jnp.concatenate(parts, axis=along)


def send_body(group_rows, tok_ref, wk_ref, wv_ref, q_ref, do_ref, owner_ref, out_ref):
    piece = tok_ref[...]
    key = dot(piece, wk_ref[...]).astype(BF16)
    value = dot(piece, wv_ref[...]).astype(BF16)
    rows = jnp.concatenate([q_ref[...], do_ref[...], key, value], axis=0)
    target = targets(owner_ref, group_rows, 1)
    shape = (out_ref.shape[0], rows.shape[0])
    select = (iota(shape, 0) == target).astype(F32).astype(BF16)
    out_ref[...] = dot(select, rows).astype(BF16)


def order_matrix(block, group_rows, transposed):
    inner = KINDS * group_rows
    sources = block // inner
    a, b = iota((block, block), 0), iota((block, block), 1)
    if transposed:
        a, b = b, a
    match = (a % sources == b // inner) & (a // sources == b % inner)
    return match.astype(F32).astype(BF16)


def attend_body(group_rows, in_ref, owner_ref, window_ref, out_ref, q_s, do_s, k_s, v_s, o_s, dq_s, dk_s, dv_s):
    devices = owner_ref.shape[0]
    inner = KINDS * group_rows
    slots, width = q_s.shape
    block = 16 * inner
    scale = 1.0 / math.sqrt(HD)
    order = order_matrix(block, group_rows, False)
    ins = (q_s, do_s, k_s, v_s)
    for b in range(devices // 16):
        part = dot(order, in_ref[b * block : (b + 1) * block, :]).astype(BF16)
        for kind in range(KINDS):
            for r in range(group_rows):
                at = (kind * group_rows + r) * 16
                ins[kind][r * devices + b * 16 : r * devices + (b + 1) * 16, :] = part[at : at + 16, :]

    sent_here = owner_ref[...] == lax.axis_index("win")
    filled = jnp.max(sent_here.astype(F32), axis=1, keepdims=True)
    window = jnp.sum(jnp.where(sent_here, window_ref[...], 0).astype(F32), axis=1, keepdims=True)
    window = jnp.where(filled > 0, window, -(iota((devices, 1), 0) + 1).astype(F32))
    wide = jnp.broadcast_to(window, (devices, devices))
    same = wide == jnp.transpose(wide)
    same = jnp.where(same, 0.0, 1.0)
    other = jnp.concatenate([jnp.concatenate([same] * group_rows, axis=1)] * group_rows, axis=0) > 0

    for h in range(width // HD):
        cols = slice(h * HD, (h + 1) * HD)
        query, dout, key, value = q_s[:, cols], do_s[:, cols], k_s[:, cols], v_s[:, cols]
        scores = jnp.where(other, -1e30, dot(query, key, NT) * scale)
        top = jnp.max(scores, axis=1, keepdims=True)
        expd = jnp.exp(scores - top)
        weights = expd / jnp.sum(expd, axis=1, keepdims=True)
        weights_low = weights.astype(BF16)
        output = dot(weights_low, value).astype(BF16)
        o_s[:, cols] = output
        dv_s[:, cols] = dot(weights_low, dout, TN).astype(BF16)
        grad_p = dot(dout, value, NT)
        delta = jnp.sum(dout.astype(F32) * output.astype(F32), axis=1, keepdims=True)
        grad_s_low = (weights * (grad_p - delta)).astype(BF16)
        dq_s[:, cols] = (dot(grad_s_low, key) * scale).astype(BF16)
        dk_s[:, cols] = (dot(grad_s_low, query, TN) * scale).astype(BF16)

    back = order_matrix(block, group_rows, True)
    outs = (o_s, dq_s, dk_s, dv_s)
    for b in range(devices // 16):
        part = jnp.concatenate(
            [
                outs[kind][r * devices + b * 16 : r * devices + (b + 1) * 16, :]
                for kind in range(KINDS)
                for r in range(group_rows)
            ],
            axis=0,
        )
        out_ref[b * block : (b + 1) * block, :] = dot(back, part).astype(BF16)


def take_body(group_rows, in_ref, owner_ref, wk_ref, wv_ref, o_ref, dq_ref, term_ref):
    tok = o_ref.shape[0]
    target = targets(owner_ref, group_rows, 0)
    shape = (KINDS * tok, in_ref.shape[0])
    select = (iota(shape, 1) == target).astype(F32).astype(BF16)
    rows = dot(select, in_ref[...]).astype(BF16)
    o_ref[...] = rows[0:tok, :]
    dq_ref[...] = rows[tok : 2 * tok, :]
    dk, dv = rows[2 * tok : 3 * tok, :], rows[3 * tok : 4 * tok, :]
    parts, _, columns = term_ref.shape
    for p in range(parts):
        at = slice(p * columns, (p + 1) * columns)
        term = dot(dk, wk_ref[at, :], NT) + dot(dv, wv_ref[at, :], NT)
        term_ref[p] = term.astype(BF16)


def local(tokens, queries, key_weight, value_weight, grad_out, owner_table, window_table):
    devices = lax.axis_size("win")
    heads = lax.axis_size("head")
    tok, columns = tokens.shape
    width = queries.shape[1]
    group_rows = tok // owner_table.shape[1]
    packed = devices * KINDS * group_rows
    slots = devices * group_rows
    params = pltpu.CompilerParams(vmem_limit_bytes=32 * 1024 * 1024)

    def call(body, outs, scratch=(), flops=1, moved=1):
        return pl.pallas_call(
            body,
            out_shape=outs,
            scratch_shapes=list(scratch),
            compiler_params=params,
            cost_estimate=pl.CostEstimate(flops=flops, bytes_accessed=moved, transcendentals=0),
        )

    def exchange(rows):
        rows = rows.reshape(devices, KINDS * group_rows, width)
        rows = lax.all_to_all(rows, "win", split_axis=0, concat_axis=0, tiled=True)
        return rows.reshape(packed, width)

    piece = lax.all_gather(tokens, "head", axis=1, tiled=True)
    sent = call(
        lambda *refs: send_body(group_rows, *refs),
        jax.ShapeDtypeStruct((packed, width), BF16),
    )(piece, key_weight, value_weight, queries, grad_out, owner_table)
    arrived = exchange(sent)
    results = call(
        lambda *refs: attend_body(group_rows, *refs),
        jax.ShapeDtypeStruct((packed, width), BF16),
        [pltpu.VMEM((slots, width), BF16)] * 8,
    )(arrived, owner_table, window_table)
    returned = exchange(results)
    attended, grad_queries, term = call(
        lambda *refs: take_body(group_rows, *refs),
        (
            jax.ShapeDtypeStruct((tok, width), BF16),
            jax.ShapeDtypeStruct((tok, width), BF16),
            jax.ShapeDtypeStruct((heads, tok, columns), BF16),
        ),
    )(returned, owner_table, key_weight, value_weight)
    terms = lax.all_to_all(term, "head", split_axis=0, concat_axis=0, tiled=True)
    grad_tokens = jnp.sum(terms.astype(F32), axis=0).astype(BF16)
    return (attended, grad_queries, grad_tokens)


def solution(mesh):
    in_specs = (
        P("win", "head"),
        P("win", "head"),
        P(None, "head"),
        P(None, "head"),
        P("win", "head"),
        P(),
        P(),
    )
    out_specs = (P("win", "head"), P("win", "head"), P("win", "head"))
    return jax.shard_map(local, mesh=mesh, in_specs=in_specs, out_specs=out_specs, check_vma=False)
```

time: 214 us -> 120 us (0.56)
  the two profiles are of different devices: /device:TPU:2 before, /device:TPU:8 now
where the time goes in v1:
time: 120 us; the launch traced here: 119 us
  blocking collectives  59.3 us (49%)
  waiting for transfers between devices  25.7 us (21%)
  starting transfers between devices  17.4 us (14%)
  Pallas kernels  7.85 us (7%)
  local copies, waits for them, and re-layouts  7.37 us (6%)
    all_to_all x1, blocking collectives, exchange(): rows = lax.all_to_all(rows, 'win', split_axis=0, concat_axis=0, tiled=True)  31.5 us
    all_to_all x1, waiting for transfers between devices, exchange(): rows = lax.all_to_all(rows, 'win', split_axis=0, concat_axis=0, tiled=True)  25.7 us
    all_to_all x1, starting transfers between devices, exchange(): rows = lax.all_to_all(rows, 'win', split_axis=0, concat_axis=0, tiled=True)  17.4 us
    all_to_all x1, blocking collectives, local(): lax.all_to_all(term, 'head', split_axis=0, concat_axis=0, tiled=True)  14 us
    all_gather x1, blocking collectives, local(): piece = lax.all_gather(tokens, 'head', axis=1, tiled=True)  13.8 us
    unnamed x16, local copies, waits for them, and re-layouts  7.37 us
    pallas_call x1, Pallas kernels, local(): call(lambda *refs: attend_body(group_rows, *refs), jax.ShapeDtypeStruct((...  2.76 us
    pallas_call x1, Pallas kernels, local(): call(lambda *refs: take_body(group_rows, *refs), (jax.ShapeDtypeStruct((t...  2.68 us
  transfers between devices with their start and end apart: 1, of which 1 were waited for; matrix products, arithmetic and copies ran while one was open for 0% of the time, Pallas kernels for 0%

profile of v1, /device:TPU:8, one launch (start us, length us, event | category | flops | bytes accessed | tf_op | source)
XLA Modules:
  0.0 119.1 jit_solution(7175117685522398478)
XLA Ops:
  0.6 0.8 copy.10.refs_5_.refs_1_
  1.5 13.8 %all_gather.3.refs_0_ = bf16[128,2560]{1,0:T(8,128)(2,1)S(1)} all-gather(bf16[128,640]{1,0:T(8,128)(2,1)} %param.7), channel_id=1, replica_groups=mesh['win'=128,'head'=4] {'head'}, dimensions={1}, use_global_device_ids=true | all-gather | bytes 819200 | tf_op jit(solution)/shard_map/all_gather | solution.py:162
  15.3 0.0 copy-start
  15.3 1.5 %copy-done = bf16[2560,384]{1,0:T(8,128)(2,1)S(1)} copy-done((bf16[2560,384]{1,0:T(8,128)(2,1)S(1)}, bf16[2560,384]{1,0:T(8,128)(2,1)}, u32[]{:S(2)}) %copy-start) | copy-done | bytes 1966104
  16.8 0.0 copy-start.2
  16.8 1.5 %copy-done.2 = bf16[2560,384]{1,0:T(8,128)(2,1)S(1)} copy-done((bf16[2560,384]{1,0:T(8,128)(2,1)S(1)}, bf16[2560,384]{1,0:T(8,128)(2,1)}, u32[]{:S(2)}) %copy-start.2) | copy-done | bytes 1966104
  18.4 0.0 copy-start.4
  18.4 0.9 copy-done.4
  19.3 0.0 copy-start.5
  19.3 0.9 copy-done.5
  20.1 0.0 copy-start.6
  20.1 2.4 %shard_map.94 = bf16[1024,384]{1,0:T(8,128)(2,1)} custom-call(bf16[128,2560]{1,0:T(8,128)(2,1)S(1)} %all_gather.3.refs_0_, bf16[2560,384]{1,0:T(8,128)(2,1)S(1)} %copy-done, bf16[2560,384]{1,0:T(8,128)(2,1)S(1)} %copy-done.2, bf16[128,384]{1,0:T(8,128)(2,1)S(1)} %copy-done.4, bf16[128,384]{1,0:T(8,128)(2,1)S(1)} %copy-done.5, s32[128,64]{1,0:T(8,128)S(1)} %copy.10.refs_5_.refs_1_), custom_call_target="tpu_custom_call" | custom-call | flops 1 | bytes 1 | tf_op jit(solution)/shard_map/pallas_call | solution.py:163
  22.6 17.4 %all-to-all-start = ((bf16[128,8,384]{2,1,0:T(8,128)(2,1)}), bf16[128,8,384]{2,1,0:T(8,128)(2,1)S(1)}, u32[]{:S(2)}, u32[]{:S(2)}) async-start(bf16[128,8,384]{2,1,0:T(8,128)(2,1)} %bitcast), calls=%async_computation | async-start | bytes 1572864 | tf_op jit(solution)/shard_map/all_to_all | solution.py:159
  39.9 0.0 copy-done.6
  39.9 0.0 copy-start.1
  40.0 0.1 copy.12.refs_2_
  40.1 25.7 %all-to-all-done = bf16[128,8,384]{2,1,0:T(8,128)(2,1)S(1)} async-done(((bf16[128,8,384]{2,1,0:T(8,128)(2,1)}), bf16[128,8,384]{2,1,0:T(8,128)(2,1)S(1)}, u32[]{:S(2)}, u32[]{:S(2)}) %all-to-all-start) | async-done | bytes 786464 | tf_op jit(solution)/shard_map/all_to_all | solution.py:159
  65.8 2.8 %shard_map.95 = bf16[1024,384]{1,0:T(8,128)(2,1)S(1)} custom-call(bf16[1024,384]{1,0:T(8,128)(2,1)S(1)} %bitcast.5, s32[128,64]{1,0:T(8,128)S(1)} %copy.10.refs_5_.refs_1_, s32[128,64]{1,0:T(8,128)S(1)} %copy.12.refs_2_), custom_call_target="tpu_custom_call" | custom-call | flops 1 | bytes 1 | tf_op jit(solution)/shard_map/pallas_call | solution.py:168
  68.5 31.5 %all_to_all.15 = bf16[128,8,384]{2,1,0:T(8,128)(2,1)S(1)} all-to-all(bf16[128,8,384]{2,1,0:T(8,128)(2,1)S(1)} %bitcast.6), channel_id=1, replica_groups=mesh['win'=128,'head'=4] {'win'}, dimensions={0} | all-to-all | bytes 1572864 | tf_op jit(solution)/shard_map/all_to_all | solution.py:159
  100.0 0.0 copy-done.1
  100.0 0.0 copy-start.3
  100.0 1.5 %copy-done.3 = bf16[2560,384]{1,0:T(8,128)(2,1)S(1)} copy-done((bf16[2560,384]{1,0:T(8,128)(2,1)S(1)}, bf16[2560,384]{1,0:T(8,128)(2,1)}, u32[]{:S(2)}) %copy-start.3) | copy-done | bytes 1966104
  101.6 2.7 %shard_map.96 = (bf16[128,384]{1,0:T(8,128)(2,1)}, bf16[128,384]{1,0:T(8,128)(2,1)}, bf16[4,128,640]{2,1,0:T(8,128)(2,1)S(1)}) custom-call(bf16[1024,384]{1,0:T(8,128)(2,1)S(1)} %bitcast.4, s32[128,64]{1,0:T(8,128)S(1)} %copy.10.refs_5_.refs_1_, bf16[2560,384]{1,0:T(8,128)(2,1)S(1)} %copy-done.1, bf16[2560,384]{1,0:T(8,128)(2,1)S(1)} %copy-done.3), custom_call_target="tpu_custom_call" | custom-call | flops 1 | bytes 1 | tf_op jit(solution)/shard_map/pallas_call | solution.py:174
  104.3 14.0 %all_to_all.16 = bf16[4,128,640]{2,1,0:T(8,128)(2,1)S(1)} all-to-all(bf16[4,128,640]{2,1,0:T(8,128)(2,1)S(1)} %get-tuple-element.8), channel_id=1, replica_groups=mesh['win'=128,'head'=4] {'head'}, dimensions={0} | all-to-all | bytes 1310720 | tf_op jit(solution)/shard_map/all_to_all | solution.py:182
  118.3 0.8 reduce_sum.12
Async XLA Ops:
  15.3 1.5 %copy-start = (bf16[2560,384]{1,0:T(8,128)(2,1)S(1)}, bf16[2560,384]{1,0:T(8,128)(2,1)}, u32[]{:S(2)}) copy-start(bf16[2560,384]{1,0:T(8,128)(2,1)} %refs_2_.4) | copy-start | bytes 5898244
  16.8 1.5 %copy-start.2 = (bf16[2560,384]{1,0:T(8,128)(2,1)S(1)}, bf16[2560,384]{1,0:T(8,128)(2,1)}, u32[]{:S(2)}) copy-start(bf16[2560,384]{1,0:T(8,128)(2,1)} %refs_3_.3) | copy-start | bytes 5898244
  18.4 0.9 copy-start.4
  19.3 0.9 copy-start.5
  20.1 19.8 %copy-start.6 = (s32[128,64]{0,1:T(8,128)S(1)}, s32[128,64]{0,1:T(8,128)}, u32[]{:S(2)}) copy-start(s32[128,64]{0,1:T(8,128)} %param.13) | copy-start | bytes 98308
  22.6 43.2 %all-to-all-start = ((bf16[128,8,384]{2,1,0:T(8,128)(2,1)}), bf16[128,8,384]{2,1,0:T(8,128)(2,1)S(1)}, u32[]{:S(2)}, u32[]{:S(2)}) async-start(bf16[128,8,384]{2,1,0:T(8,128)(2,1)} %bitcast), calls=%async_computation | async-start | bytes 1572864 | tf_op jit(solution)/shard_map/all_to_all | solution.py:159
  39.9 60.1 %copy-start.1 = (bf16[2560,384]{1,0:T(8,128)(2,1)S(1)}, bf16[2560,384]{1,0:T(8,128)(2,1)}, u32[]{:S(2)}) copy-start(bf16[2560,384]{1,0:T(8,128)(2,1)} %refs_2_.4) | copy-start | bytes 5898244
  100.0 1.5 %copy-start.3 = (bf16[2560,384]{1,0:T(8,128)(2,1)S(1)}, bf16[2560,384]{1,0:T(8,128)(2,1)}, u32[]{:S(2)}) copy-start(bf16[2560,384]{1,0:T(8,128)(2,1)} %refs_3_.3) | copy-start | bytes 5898244

commit v2 on v1

v2 whole, which is shorter than its diff:
```python
import math

import jax
import jax.numpy as jnp
from jax import lax
from jax.experimental import pallas as pl
from jax.experimental.pallas import tpu as pltpu
from jax.sharding import PartitionSpec as P

HD = 128
KINDS = 4
F32 = jnp.float32
BF16 = jnp.bfloat16
NN = (((1,), (0,)), ((), ()))
NT = (((1,), (1,)), ((), ()))
TN = (((0,), (0,)), ((), ()))


def dot(a, b, dims=NN):
    return lax.dot_general(a, b, dims, preferred_element_type=F32)


def iota(shape, dim):
    return lax.broadcasted_iota(jnp.int32, shape, dim)


def targets(owner_ref, group_rows):
    picks, devices = owner_ref.shape
    tok = picks * group_rows
    here = iota((picks, devices), 1) == lax.axis_index("win")
    own = jnp.sum(jnp.where(here, owner_ref[...], 0).astype(F32), axis=1, keepdims=True)
    spread = iota((picks, tok), 1) // group_rows == iota((picks, tok), 0)
    own = jnp.sum(jnp.where(spread, own, 0.0), axis=0, keepdims=True)
    inner = (iota((1, tok), 1) % group_rows).astype(F32)
    return own * (KINDS * group_rows) + inner


def start_weights(wk_hbm, wv_hbm, wk_s, wv_s, sems, chunks):
    rows = wk_s.shape[0] // chunks
    copies = []
    for c in range(chunks):
        at = pl.ds(c * rows, rows)
        pair = (
            pltpu.make_async_copy(wk_hbm.at[at], wk_s.at[at], sems.at[2 * c]),
            pltpu.make_async_copy(wv_hbm.at[at], wv_s.at[at], sems.at[2 * c + 1]),
        )
        pair[0].start()
        pair[1].start()
        copies.append(pair)
    return copies


def send_body(
    group_rows,
    tok_ref,
    owner_hbm,
    q_hbm,
    do_hbm,
    wk_hbm,
    wv_hbm,
    out_ref,
    owner_s,
    rows_s,
    wk_s,
    wv_s,
    sems,
):
    tok = tok_ref.shape[0]
    chunks = (sems.shape[0] - 3) // 2
    copy_owner = pltpu.make_async_copy(owner_hbm, owner_s, sems.at[2 * chunks + 2])
    copy_owner.start()
    copies = start_weights(wk_hbm, wv_hbm, wk_s, wv_s, sems, chunks)
    copy_q = pltpu.make_async_copy(q_hbm, rows_s.at[pl.ds(0, tok)], sems.at[2 * chunks])
    copy_do = pltpu.make_async_copy(do_hbm, rows_s.at[pl.ds(tok, tok)], sems.at[2 * chunks + 1])
    copy_q.start()
    copy_do.start()
    copy_owner.wait()
    target = targets(owner_s, group_rows)
    target = jnp.concatenate([target + kind * group_rows for kind in range(KINDS)], axis=1)
    shape = (out_ref.shape[0], KINDS * tok)
    select = (iota(shape, 0) == target.astype(jnp.int32)).astype(F32).astype(BF16)
    rows = wk_s.shape[0] // chunks
    key = value = None
    for c, (copy_k, copy_v) in enumerate(copies):
        at = slice(c * rows, (c + 1) * rows)
        copy_k.wait()
        part = dot(tok_ref[:, at], wk_s[at, :])
        key = part if key is None else key + part
        copy_v.wait()
        part = dot(tok_ref[:, at], wv_s[at, :])
        value = part if value is None else value + part
    rows_s[2 * tok : 3 * tok, :] = key.astype(BF16)
    rows_s[3 * tok : 4 * tok, :] = value.astype(BF16)
    copy_q.wait()
    copy_do.wait()
    out_ref[...] = dot(select, rows_s[...]).astype(BF16)


def order_matrix(block, group_rows, transposed):
    inner = KINDS * group_rows
    sources = block // inner
    a, b = iota((block, block), 0), iota((block, block), 1)
    if transposed:
        a, b = b, a
    match = (a % sources == b // inner) & (a // sources == b % inner)
    return match.astype(F32).astype(BF16)


def attend_body(group_rows, in_ref, owner_ref, window_ref, out_ref, q_s, do_s, k_s, v_s, o_s, dq_s, dk_s, dv_s):
    devices = owner_ref.shape[1]
    inner = KINDS * group_rows
    slots, width = q_s.shape
    block = 16 * inner
    scale = 1.0 / math.sqrt(HD)
    order = order_matrix(block, group_rows, False)
    ins = (q_s, do_s, k_s, v_s)
    for b in range(devices // 16):
        part = dot(order, in_ref[b * block : (b + 1) * block, :]).astype(BF16)
        for kind in range(KINDS):
            for r in range(group_rows):
                at = (kind * group_rows + r) * 16
                ins[kind][r * devices + b * 16 : r * devices + (b + 1) * 16, :] = part[at : at + 16, :]

    sent_here = owner_ref[...] == lax.axis_index("win")
    filled = jnp.max(sent_here.astype(F32), axis=0, keepdims=True)
    window = jnp.sum(jnp.where(sent_here, window_ref[...], 0).astype(F32), axis=0, keepdims=True)
    window = jnp.where(filled > 0, window, -(iota((1, devices), 1) + 1).astype(F32))
    wide = jnp.broadcast_to(window, (devices, devices))
    same = wide == jnp.transpose(wide)
    same = jnp.where(same, 0.0, 1.0)
    other = jnp.concatenate([jnp.concatenate([same] * group_rows, axis=1)] * group_rows, axis=0) > 0

    for h in range(width // HD):
        cols = slice(h * HD, (h + 1) * HD)
        query, dout, key, value = q_s[:, cols], do_s[:, cols], k_s[:, cols], v_s[:, cols]
        scores = jnp.where(other, -1e30, dot(query, key, NT) * scale)
        top = jnp.max(scores, axis=1, keepdims=True)
        expd = jnp.exp(scores - top)
        weights = expd / jnp.sum(expd, axis=1, keepdims=True)
        weights_low = weights.astype(BF16)
        output = dot(weights_low, value).astype(BF16)
        o_s[:, cols] = output
        dv_s[:, cols] = dot(weights_low, dout, TN).astype(BF16)
        grad_p = dot(dout, value, NT)
        delta = jnp.sum(dout.astype(F32) * output.astype(F32), axis=1, keepdims=True)
        grad_s_low = (weights * (grad_p - delta)).astype(BF16)
        dq_s[:, cols] = (dot(grad_s_low, key) * scale).astype(BF16)
        dk_s[:, cols] = (dot(grad_s_low, query, TN) * scale).astype(BF16)

    back = order_matrix(block, group_rows, True)
    outs = (o_s, dq_s, dk_s, dv_s)
    for b in range(devices // 16):
        part = jnp.concatenate(
            [
                outs[kind][r * devices + b * 16 : r * devices + (b + 1) * 16, :]
                for kind in range(KINDS)
                for r in range(group_rows)
            ],
            axis=0,
        )
        out_ref[b * block : (b + 1) * block, :] = dot(back, part).astype(BF16)


def take_body(
    group_rows, in_ref, owner_ref, wk_ref, wv_ref, o_hbm, dq_hbm, term_ref, rows_s, sems
):
    parts, tok, columns = term_ref.shape
    target = targets(owner_ref, group_rows)
    target = jnp.transpose(jnp.broadcast_to(target, (tok, tok)))[:, 0:1]
    target = jnp.concatenate([target + kind * group_rows for kind in range(KINDS)], axis=0)
    shape = (KINDS * tok, in_ref.shape[0])
    select = (iota(shape, 1) == target.astype(jnp.int32)).astype(F32).astype(BF16)
    rows_s[...] = dot(select, in_ref[...]).astype(BF16)
    copy_o = pltpu.make_async_copy(rows_s.at[pl.ds(0, tok)], o_hbm, sems.at[0])
    copy_dq = pltpu.make_async_copy(rows_s.at[pl.ds(tok, tok)], dq_hbm, sems.at[1])
    copy_o.start()
    copy_dq.start()
    dk, dv = rows_s[2 * tok : 3 * tok, :], rows_s[3 * tok : 4 * tok, :]
    for p in range(parts):
        at = slice(p * columns, (p + 1) * columns)
        term = dot(dk, wk_ref[at, :], NT) + dot(dv, wv_ref[at, :], NT)
        term_ref[p] = term.astype(BF16)
    copy_o.wait()
    copy_dq.wait()


def local(tokens, queries, key_weight, value_weight, grad_out, owner_table, window_table):
    devices = lax.axis_size("win")
    heads = lax.axis_size("head")
    tok, columns = tokens.shape
    width = queries.shape[1]
    group_rows = tok // owner_table.shape[1]
    packed = devices * KINDS * group_rows
    slots = devices * group_rows

    vmem = pl.BlockSpec(memory_space=pltpu.VMEM)
    hbm = pl.BlockSpec(memory_space=pltpu.HBM)

    def call(body, outs, in_specs, out_specs, scratch):
        return pl.pallas_call(
            lambda *refs: body(group_rows, *refs),
            out_shape=outs,
            in_specs=in_specs,
            out_specs=out_specs,
            scratch_shapes=scratch,
            compiler_params=pltpu.CompilerParams(vmem_limit_bytes=32 << 20),
        )

    def exchange(rows):
        rows = rows.reshape(devices, KINDS * group_rows, width)
        rows = lax.all_to_all(rows, "win", split_axis=0, concat_axis=0, tiled=True)
        return rows.reshape(packed, width)

    owners, windows = owner_table.T, window_table.T
    packed_rows = jax.ShapeDtypeStruct((packed, width), BF16)
    token_rows = jax.ShapeDtypeStruct((tok, width), BF16)
    piece = lax.all_gather(tokens, "head", axis=1, tiled=True)
    stay = [
        pltpu.with_memory_space_constraint(array, pltpu.HBM)
        for array in (owners, queries, grad_out, key_weight, value_weight)
    ]
    sent = call(
        send_body,
        packed_rows,
        [vmem] + [hbm] * len(stay),
        vmem,
        [
            pltpu.VMEM(owners.shape, jnp.int32),
            pltpu.VMEM((KINDS * tok, width), BF16),
            pltpu.VMEM(key_weight.shape, BF16),
            pltpu.VMEM(key_weight.shape, BF16),
            pltpu.SemaphoreType.DMA((11,)),
        ],
    )(piece, *stay)
    arrived = exchange(sent)
    results = call(
        attend_body, packed_rows, [vmem] * 3, vmem, [pltpu.VMEM((slots, width), BF16)] * 8
    )(arrived, owners, windows)
    returned = exchange(results)
    attended, grad_queries, term = call(
        take_body,
        (token_rows, token_rows, jax.ShapeDtypeStruct((heads, tok, columns), BF16)),
        [vmem] * 4,
        (hbm, hbm, vmem),
        [pltpu.VMEM((KINDS * tok, width), BF16), pltpu.SemaphoreType.DMA((2,))],
    )(returned, owners, key_weight, value_weight)
    terms = lax.all_to_all(term, "head", split_axis=0, concat_axis=0, tiled=True)
    grad_tokens = jnp.sum(terms.astype(F32), axis=0).astype(BF16)
    return (attended, grad_queries, grad_tokens)


def solution(mesh):
    in_specs = (
        P("win", "head"),
        P("win", "head"),
        P(None, "head"),
        P(None, "head"),
        P("win", "head"),
        P(),
        P(),
    )
    out_specs = (P("win", "head"), P("win", "head"), P("win", "head"))
    return jax.shard_map(local, mesh=mesh, in_specs=in_specs, out_specs=out_specs, check_vma=False)
```

time: 120 us -> 113 us (0.942)
  blocking collectives: 59.3 us -> 102 us
  waiting for transfers between devices: 25.7 us -> 0 us
  starting transfers between devices: 17.4 us -> 0 us
  local copies, waits for them, and re-layouts: 7.37 us -> 0.02 us
  Pallas kernels: 7.85 us -> 9.35 us
    all_to_all x1 -> x2, blocking collectives: 31.5 us -> 74.6 us  [exchange(): rows = lax.all_to_all(rows, 'win', split_axis=0, concat_axis=0, tiled=True)]
    all_to_all x1 -> x0, waiting for transfers between devices: 25.7 us -> none  [exchange(): rows = lax.all_to_all(rows, 'win', split_axis=0, concat_axis=0, tiled=True)]
    all_to_all x1 -> x0, starting transfers between devices: 17.4 us -> none  [exchange(): rows = lax.all_to_all(rows, 'win', split_axis=0, concat_axis=0, tiled=True)]
    unnamed x16 -> x8, local copies, waits for them, and re-layouts: 7.37 us -> 0.02 us
    pallas_call x3, Pallas kernels: 7.85 us -> 9.35 us  [the longest x1 3.68 us: local(): call(send_body, packed_rows, [vmem] + [hbm] * len(stay), vmem, [pltpu.VME...]
  transfers between devices with their start and end apart: 1 -> 0, of which waited for: 1 -> 0; matrix products, arithmetic and copies ran while one was open for 0% -> 0% of each run, Pallas kernels for 0% -> 0%
where the time goes in v2:
time: 113 us
  blocking collectives  102 us (90%)
  Pallas kernels  9.35 us (8%)
    all_to_all x2, blocking collectives, exchange(): rows = lax.all_to_all(rows, 'win', split_axis=0, concat_axis=0, tiled=True)  74.6 us
    all_to_all x1, blocking collectives, local(): lax.all_to_all(term, 'head', split_axis=0, concat_axis=0, tiled=True)  14 us
    all_gather x1, blocking collectives, local(): piece = lax.all_gather(tokens, 'head', axis=1, tiled=True)  13.8 us
    pallas_call x1, Pallas kernels, local(): call(send_body, packed_rows, [vmem] + [hbm] * len(stay), vmem, [pltpu.VME...  3.68 us
    pallas_call x1, Pallas kernels, local(): call(take_body, (token_rows, token_rows, jax.ShapeDtypeStruct((heads, tok...  2.9 us
    pallas_call x1, Pallas kernels, local(): call(attend_body, packed_rows, [vmem] * 3, vmem, [pltpu.VMEM((slots, widt...  2.77 us

profile of v2, /device:TPU:8, one launch (start us, length us, event | category | flops | bytes accessed | tf_op | source)
XLA Modules:
  0.0 113.2 jit_solution(12512665013194541299)
XLA Ops:
  0.6 13.8 %all_gather.3.refs_0_ = bf16[128,2560]{1,0:T(8,128)(2,1)S(1)} all-gather(bf16[128,640]{1,0:T(8,128)(2,1)} %param.7), channel_id=1, replica_groups=mesh['win'=128,'head'=4] {'head'}, dimensions={1}, use_global_device_ids=true | all-gather | bytes 819200 | tf_op jit(solution)/shard_map/all_gather | solution.py:217
  14.4 0.0 copy-start.2
  14.4 0.0 copy-start.3
  14.4 3.7 %shard_map.94 = bf16[1024,384]{1,0:T(8,128)(2,1)S(1)} custom-call(bf16[128,2560]{1,0:T(8,128)(2,1)S(1)} %all_gather.3.refs_0_, s32[64,128]{1,0:T(8,128)} %bitcast.10, bf16[128,384]{1,0:T(8,128)(2,1)} %refs_2_.2, bf16[128,384]{1,0:T(8,128)(2,1)} %refs_3_.2, bf16[2560,384]{1,0:T(8,128)(2,1)} %refs_2_.3, bf16[2560,384]{1,0:T(8,128)(2,1)} %refs_3_.3), custom_call_target="tpu_custom_call" | custom-call | tf_op jit(solution)/shard_map/pallas_call | solution.py:222
  18.1 0.0 copy-start.1
  18.1 43.1 %all_to_all.15 = bf16[128,8,384]{2,1,0:T(8,128)(2,1)S(1)} all-to-all(bf16[128,8,384]{2,1,0:T(8,128)(2,1)S(1)} %bitcast.9), channel_id=1, replica_groups=mesh['win'=128,'head'=4] {'win'}, dimensions={0} | all-to-all | bytes 1572864 | tf_op jit(solution)/shard_map/all_to_all | solution.py:211
  61.3 0.0 copy-start
  61.3 0.0 copy-done.2
  61.3 0.0 copy-done.3
  61.3 2.8 %shard_map.95 = bf16[1024,384]{1,0:T(8,128)(2,1)S(1)} custom-call(bf16[1024,384]{1,0:T(8,128)(2,1)S(1)} %bitcast.7, s32[64,128]{1,0:T(8,128)S(1)} %bitcast.11, s32[64,128]{1,0:T(8,128)S(1)} %bitcast.13), custom_call_target="tpu_custom_call" | custom-call | tf_op jit(solution)/shard_map/pallas_call | solution.py:236
  64.0 31.5 %all_to_all.16 = bf16[128,8,384]{2,1,0:T(8,128)(2,1)S(1)} all-to-all(bf16[128,8,384]{2,1,0:T(8,128)(2,1)S(1)} %bitcast.8), channel_id=1, replica_groups=mesh['win'=128,'head'=4] {'win'}, dimensions={0} | all-to-all | bytes 1572864 | tf_op jit(solution)/shard_map/all_to_all | solution.py:211
  95.5 0.0 copy-done.1
  95.5 0.0 copy-done
  95.5 2.9 %shard_map.96 = (bf16[128,384]{1,0:T(8,128)(2,1)}, bf16[128,384]{1,0:T(8,128)(2,1)}, bf16[4,128,640]{2,1,0:T(8,128)(2,1)S(1)}) custom-call(bf16[1024,384]{1,0:T(8,128)(2,1)S(1)} %bitcast.6, s32[64,128]{1,0:T(8,128)S(1)} %bitcast.12, bf16[2560,384]{1,0:T(8,128)(2,1)S(1)} %copy-done, bf16[2560,384]{1,0:T(8,128)(2,1)S(1)} %copy-done.1), custom_call_target="tpu_custom_call" | custom-call | tf_op jit(solution)/shard_map/pallas_call | solution.py:240
  98.5 14.0 %all_to_all.17 = bf16[4,128,640]{2,1,0:T(8,128)(2,1)S(1)} all-to-all(bf16[4,128,640]{2,1,0:T(8,128)(2,1)S(1)} %get-tuple-element.8), channel_id=1, replica_groups=mesh['win'=128,'head'=4] {'head'}, dimensions={0} | all-to-all | bytes 1310720 | tf_op jit(solution)/shard_map/all_to_all | solution.py:247
  112.5 0.8 reduce_sum.12
Async XLA Ops:
  14.4 46.9 %copy-start.2 = (s32[128,64]{0,1:T(8,128)S(1)}, s32[128,64]{0,1:T(8,128)}, u32[]{:S(2)}) copy-start(s32[128,64]{0,1:T(8,128)} %param.12) | copy-start | bytes 98308
  14.4 46.9 %copy-start.3 = (s32[128,64]{0,1:T(8,128)S(1)}, s32[128,64]{0,1:T(8,128)}, u32[]{:S(2)}) copy-start(s32[128,64]{0,1:T(8,128)} %param.13) | copy-start | bytes 98308
  18.1 77.4 %copy-start.1 = (bf16[2560,384]{1,0:T(8,128)(2,1)S(1)}, bf16[2560,384]{1,0:T(8,128)(2,1)}, u32[]{:S(2)}) copy-start(bf16[2560,384]{1,0:T(8,128)(2,1)} %refs_3_.3) | copy-start | bytes 5898244
  61.3 34.3 %copy-start = (bf16[2560,384]{1,0:T(8,128)(2,1)S(1)}, bf16[2560,384]{1,0:T(8,128)(2,1)}, u32[]{:S(2)}) copy-start(bf16[2560,384]{1,0:T(8,128)(2,1)} %refs_2_.3) | copy-start | bytes 5898244

commit v3 on v2

--- a/solution.py
+++ b/solution.py
@@ -35,65 +35,43 @@
     return own * (KINDS * group_rows) + inner
 
 
-def start_weights(wk_hbm, wv_hbm, wk_s, wv_s, sems, chunks):
-    rows = wk_s.shape[0] // chunks
-    copies = []
-    for c in range(chunks):
-        at = pl.ds(c * rows, rows)
-        pair = (
-            pltpu.make_async_copy(wk_hbm.at[at], wk_s.at[at], sems.at[2 * c]),
-            pltpu.make_async_copy(wv_hbm.at[at], wv_s.at[at], sems.at[2 * c + 1]),
-        )
-        pair[0].start()
-        pair[1].start()
-        copies.append(pair)
-    return copies
-
-
-def send_body(
-    group_rows,
-    tok_ref,
-    owner_hbm,
-    q_hbm,
-    do_hbm,
-    wk_hbm,
-    wv_hbm,
-    out_ref,
-    owner_s,
-    rows_s,
-    wk_s,
-    wv_s,
-    sems,
-):
-    tok = tok_ref.shape[0]
-    chunks = (sems.shape[0] - 3) // 2
-    copy_owner = pltpu.make_async_copy(owner_hbm, owner_s, sems.at[2 * chunks + 2])
+def select_rows(owner_ref, group_rows, kinds, shape):
+    target = targets(owner_ref, group_rows)
+    target = jnp.concatenate([target + kind * group_rows for kind in kinds], axis=1)
+    return (iota(shape, 0) == target.astype(jnp.int32)).astype(F32).astype(BF16)
+
+
+def pack_body(group_rows, owner_hbm, q_hbm, do_hbm, pack_ref, owner_s, rows_s, sems):
+    tok = q_hbm.shape[0]
+    copy_owner = pltpu.make_async_copy(owner_hbm, owner_s, sems.at[0])
+    copy_q = pltpu.make_async_copy(q_hbm, rows_s.at[pl.ds(0, tok)], sems.at[1])
+    copy_do = pltpu.make_async_copy(do_hbm, rows_s.at[pl.ds(tok, tok)], sems.at[2])
     copy_owner.start()
-    copies = start_weights(wk_hbm, wv_hbm, wk_s, wv_s, sems, chunks)
-    copy_q = pltpu.make_async_copy(q_hbm, rows_s.at[pl.ds(0, tok)], sems.at[2 * chunks])
-    copy_do = pltpu.make_async_copy(do_hbm, rows_s.at[pl.ds(tok, tok)], sems.at[2 * chunks + 1])
     copy_q.start()
     copy_do.start()
     copy_owner.wait()
-    target = targets(owner_s, group_rows)
-    target = jnp.concatenate([target + kind * group_rows for kind in range(KINDS)], axis=1)
-    shape = (out_ref.shape[0], KINDS * tok)
-    select = (iota(shape, 0) == target.astype(jnp.int32)).astype(F32).astype(BF16)
-    rows = wk_s.shape[0] // chunks
-    key = value = None
-    for c, (copy_k, copy_v) in enumerate(copies):
-        at = slice(c * rows, (c + 1) * rows)
-        copy_k.wait()
-        part = dot(tok_ref[:, at], wk_s[at, :])
-        key = part if key is None else key + part
-        copy_v.wait()
-        part = dot(tok_ref[:, at], wv_s[at, :])
-        value = part if value is None else value + part
-    rows_s[2 * tok : 3 * tok, :] = key.astype(BF16)
-    rows_s[3 * tok : 4 * tok, :] = value.astype(BF16)
+    select = select_rows(owner_s, group_rows, (0, 1), (pack_ref.shape[0], 2 * tok))
     copy_q.wait()
     copy_do.wait()
-    out_ref[...] = dot(select, rows_s[...]).astype(BF16)
+    pack_ref[...] = dot(select, rows_s[...]).astype(BF16)
+
+
+def send_body(group_rows, tok_ref, pack_ref, owner_ref, wk_ref, wv_hbm, out_ref, wv_s, sem):
+    parts, tok, columns = tok_ref.shape
+    copy_v = pltpu.make_async_copy(wv_hbm, wv_s, sem)
+    copy_v.start()
+    select = select_rows(owner_ref, group_rows, (2, 3), (out_ref.shape[0], 2 * tok))
+
+    def project(weight_ref):
+        total = dot(tok_ref[0], weight_ref[0:columns, :])
+        for p in range(1, parts):
+            total = total + dot(tok_ref[p], weight_ref[p * columns : (p + 1) * columns, :])
+        return total.astype(BF16)
+
+    key = project(wk_ref)
+    copy_v.wait()
+    rows = jnp.concatenate([key, project(wv_s)], axis=0)
+    out_ref[...] = (pack_ref[...].astype(F32) + dot(select, rows)).astype(BF16)
 
 
 def order_matrix(block, group_rows, transposed):
@@ -161,27 +139,31 @@
         out_ref[b * block : (b + 1) * block, :] = dot(back, part).astype(BF16)
 
 
-def take_body(
-    group_rows, in_ref, owner_ref, wk_ref, wv_ref, o_hbm, dq_hbm, term_ref, rows_s, sems
-):
-    parts, tok, columns = term_ref.shape
+def taken(group_rows, in_ref, owner_ref, kinds):
+    tok = owner_ref.shape[0] * group_rows
     target = targets(owner_ref, group_rows)
     target = jnp.transpose(jnp.broadcast_to(target, (tok, tok)))[:, 0:1]
-    target = jnp.concatenate([target + kind * group_rows for kind in range(KINDS)], axis=0)
-    shape = (KINDS * tok, in_ref.shape[0])
+    target = jnp.concatenate([target + kind * group_rows for kind in kinds], axis=0)
+    shape = (len(kinds) * tok, in_ref.shape[0])
     select = (iota(shape, 1) == target.astype(jnp.int32)).astype(F32).astype(BF16)
-    rows_s[...] = dot(select, in_ref[...]).astype(BF16)
-    copy_o = pltpu.make_async_copy(rows_s.at[pl.ds(0, tok)], o_hbm, sems.at[0])
-    copy_dq = pltpu.make_async_copy(rows_s.at[pl.ds(tok, tok)], dq_hbm, sems.at[1])
-    copy_o.start()
-    copy_dq.start()
-    dk, dv = rows_s[2 * tok : 3 * tok, :], rows_s[3 * tok : 4 * tok, :]
+    return dot(select, in_ref[...]).astype(BF16)
+
+
+def term_body(group_rows, in_ref, owner_ref, wk_ref, wv_ref, term_ref):
+    parts, tok, columns = term_ref.shape
+    rows = taken(group_rows, in_ref, owner_ref, (2, 3))
+    dk, dv = rows[:tok, :], rows[tok:, :]
     for p in range(parts):
         at = slice(p * columns, (p + 1) * columns)
         term = dot(dk, wk_ref[at, :], NT) + dot(dv, wv_ref[at, :], NT)
         term_ref[p] = term.astype(BF16)
-    copy_o.wait()
-    copy_dq.wait()
+
+
+def take_body(group_rows, in_ref, owner_ref, o_ref, dq_ref):
+    tok = o_ref.shape[0]
+    rows = taken(group_rows, in_ref, owner_ref, (0, 1))
+    o_ref[...] = rows[:tok, :]
+    dq_ref[...] = rows[tok:, :]
 
 
 def local(tokens, queries, key_weight, value_weight, grad_out, owner_table, window_table):
@@ -214,36 +196,41 @@
     owners, windows = owner_table.T, window_table.T
     packed_rows = jax.ShapeDtypeStruct((packed, width), BF16)
     token_rows = jax.ShapeDtypeStruct((tok, width), BF16)
-    piece = lax.all_gather(tokens, "head", axis=1, tiled=True)
-    stay = [
+    copies = jnp.broadcast_to(tokens[None], (heads, tok, columns))
+    piece = lax.all_to_all(copies, "head", split_axis=0, concat_axis=0, tiled=True)
+    owners_hbm, queries, grad_out, value_hbm = (
         pltpu.with_memory_space_constraint(array, pltpu.HBM)
-        for array in (owners, queries, grad_out, key_weight, value_weight)
-    ]
+        for array in (owners, queries, grad_out, value_weight)
+    )
+    pack = call(
+        pack_body,
+        packed_rows,
+        [hbm] * 3,
+        vmem,
+        [
+            pltpu.VMEM(owners.shape, jnp.int32),
+            pltpu.VMEM((2 * tok, width), BF16),
+            pltpu.SemaphoreType.DMA((3,)),
+        ],
+    )(owners_hbm, queries, grad_out)
     sent = call(
         send_body,
         packed_rows,
-        [vmem] + [hbm] * len(stay),
+        [vmem] * 4 + [hbm],
         vmem,
-        [
-            pltpu.VMEM(owners.shape, jnp.int32),
-            pltpu.VMEM((KINDS * tok, width), BF16),
-            pltpu.VMEM(key_weight.shape, BF16),
-            pltpu.VMEM(key_weight.shape, BF16),
-            pltpu.SemaphoreType.DMA((11,)),
-        ],
-    )(piece, *stay)
+        [pltpu.VMEM(value_weight.shape, BF16), pltpu.SemaphoreType.DMA],
+    )(piece, pack, owners, key_weight, value_hbm)
     arrived = exchange(sent)
     results = call(
         attend_body, packed_rows, [vmem] * 3, vmem, [pltpu.VMEM((slots, width), BF16)] * 8
     )(arrived, owners, windows)
     returned = exchange(results)
-    attended, grad_queries, term = call(
-        take_body,
-        (token_rows, token_rows, jax.ShapeDtypeStruct((heads, tok, columns), BF16)),
-        [vmem] * 4,
-        (hbm, hbm, vmem),
-        [pltpu.VMEM((KINDS * tok, width), BF16), pltpu.SemaphoreType.DMA((2,))],
+    term = call(
+        term_body, jax.ShapeDtypeStruct((heads, tok, columns), BF16), [vmem] * 4, vmem, []
     )(returned, owners, key_weight, value_weight)
+    attended, grad_queries = call(
+        take_body, (token_rows, token_rows), [vmem] * 2, (vmem, vmem), []
+    )(returned, owners)
     terms = lax.all_to_all(term, "head", split_axis=0, concat_axis=0, tiled=True)
     grad_tokens = jnp.sum(terms.astype(F32), axis=0).astype(BF16)
     return (attended, grad_queries, grad_tokens)

time: 113 us -> 116 us (1.027)
  blocking collectives: 102 us -> 74.5 us
  waiting for transfers between devices: 0 us -> 17.9 us
  starting transfers between devices: 0 us -> 7.77 us
  Pallas kernels: 9.35 us -> 11.5 us
  local copies, waits for them, and re-layouts: 0.02 us -> 1.97 us
    all_to_all x0 -> x2, waiting for transfers between devices: none -> 17.9 us  [the longest x1 9.41 us: local(): lax.all_to_all(copies, 'head', split_axis=0, concat_axis=0, tiled=True)]
    all_to_all x1 -> x0, blocking collectives: 14 us -> none  [local(): lax.all_to_all(term, 'head', split_axis=0, concat_axis=0, tiled=True)]
    all_gather x1 -> x0, blocking collectives: 13.8 us -> none  [local(): piece = lax.all_gather(tokens, 'head', axis=1, tiled=True)]
    all_to_all x0 -> x2, starting transfers between devices: none -> 7.77 us  [the longest x1 4.29 us: local(): lax.all_to_all(copies, 'head', split_axis=0, concat_axis=0, tiled=True)]
    pallas_call x2 -> x4, Pallas kernels: 6.58 us -> 8.76 us  [the longest x1 3.12 us: local(): call(send_body, packed_rows, [vmem] * 4 + [hbm], vmem, [pltpu.VMEM(value_...]
    broadcast_in_dim x0 -> x1, local copies, waits for them, and re-layouts: none -> 1.95 us  [local(): copies = jnp.broadcast_to(tokens[None], (heads, tok, columns))]
  transfers between devices with their start and end apart: 0 -> 2, of which waited for: 0 -> 2; matrix products, arithmetic and copies ran while one was open for 0% -> 0% of each run, Pallas kernels for 0% -> 2%
where the time goes in v3:
time: 116 us; the launch traced here: 115 us
  blocking collectives  74.5 us (64%)
  waiting for transfers between devices  17.9 us (15%)
  Pallas kernels  11.5 us (10%)
  starting transfers between devices  7.77 us (7%)
  local copies, waits for them, and re-layouts  1.97 us (2%)
    all_to_all x2, blocking collectives, exchange(): rows = lax.all_to_all(rows, 'win', split_axis=0, concat_axis=0, tiled=True)  74.5 us
    all_to_all x1, waiting for transfers between devices, local(): lax.all_to_all(copies, 'head', split_axis=0, concat_axis=0, tiled=True)  9.41 us
    all_to_all x1, waiting for transfers between devices, local(): lax.all_to_all(term, 'head', split_axis=0, concat_axis=0, tiled=True)  8.52 us
    all_to_all x1, starting transfers between devices, local(): lax.all_to_all(copies, 'head', split_axis=0, concat_axis=0, tiled=True)  4.29 us
    all_to_all x1, starting transfers between devices, local(): lax.all_to_all(term, 'head', split_axis=0, concat_axis=0, tiled=True)  3.48 us
    pallas_call x1, Pallas kernels, local(): call(send_body, packed_rows, [vmem] * 4 + [hbm], vmem, [pltpu.VMEM(value_...  3.12 us
    pallas_call x1, Pallas kernels, local(): call(term_body, jax.ShapeDtypeStruct((heads, tok, columns), BF16), [vmem]...  2.86 us
    pallas_call x1, Pallas kernels, local(): call(attend_body, packed_rows, [vmem] * 3, vmem, [pltpu.VMEM((slots, widt...  2.77 us
  transfers between devices with their start and end apart: 2, of which 2 were waited for; matrix products, arithmetic and copies ran while one was open for 0% of the time, Pallas kernels for 2%

profile of v3, /device:TPU:8, one launch (start us, length us, event | category | flops | bytes accessed | tf_op | source)
XLA Modules:
  0.0 115.2 jit_solution(2926800823617723683)
XLA Ops:
  0.6 0.0 copy-start.2
  0.6 0.0 copy-start
  0.7 1.9 %broadcast_in_dim.2 = bf16[4,128,640]{2,1,0:T(8,128)(2,1)} broadcast(bf16[128,640]{1,0:T(8,128)(2,1)} %param.7), dimensions={1,2} | broadcast | bytes 819200 | tf_op jit(solution)/shard_map/broadcast_in_dim | solution.py:199
  2.6 4.3 %all-to-all-start = ((bf16[4,128,640]{2,1,0:T(8,128)(2,1)}), bf16[4,128,640]{2,1,0:T(8,128)(2,1)S(1)}, u32[]{:S(2)}, u32[]{:S(2)}) async-start(bf16[4,128,640]{2,1,0:T(8,128)(2,1)} %broadcast_in_dim.2), calls=%async_computation | async-start | bytes 1310720 | tf_op jit(solution)/shard_map/all_to_all | solution.py:200
  6.9 1.4 %shard_map.94.refs_1_ = bf16[1024,384]{1,0:T(8,128)(2,1)S(1)} custom-call(s32[64,128]{1,0:T(8,128)} %bitcast.11, bf16[128,384]{1,0:T(8,128)(2,1)} %refs_1_.1, bf16[128,384]{1,0:T(8,128)(2,1)} %refs_2_.2), custom_call_target="tpu_custom_call" | custom-call | tf_op jit(solution)/shard_map/pallas_call | solution.py:205
  8.3 0.0 copy-start.3
  8.4 9.4 %all-to-all-done.refs_0_ = bf16[4,128,640]{2,1,0:T(8,128)(2,1)S(1)} async-done(((bf16[4,128,640]{2,1,0:T(8,128)(2,1)}), bf16[4,128,640]{2,1,0:T(8,128)(2,1)S(1)}, u32[]{:S(2)}, u32[]{:S(2)}) %all-to-all-start) | async-done | bytes 655392 | tf_op jit(solution)/shard_map/all_to_all | solution.py:200
  17.8 0.0 copy-done.2
  17.8 0.0 copy-done
  17.8 3.1 %shard_map.95 = bf16[1024,384]{1,0:T(8,128)(2,1)S(1)} custom-call(bf16[4,128,640]{2,1,0:T(8,128)(2,1)S(1)} %all-to-all-done.refs_0_, bf16[1024,384]{1,0:T(8,128)(2,1)S(1)} %shard_map.94.refs_1_, s32[64,128]{1,0:T(8,128)S(1)} %bitcast.12, bf16[2560,384]{1,0:T(8,128)(2,1)S(1)} %copy-done, bf16[2560,384]{1,0:T(8,128)(2,1)} %refs_3_.3), custom_call_target="tpu_custom_call" | custom-call | tf_op jit(solution)/shard_map/pallas_call | solution.py:216
  20.9 43.0 %all_to_all.20 = bf16[128,8,384]{2,1,0:T(8,128)(2,1)S(1)} all-to-all(bf16[128,8,384]{2,1,0:T(8,128)(2,1)S(1)} %bitcast.8), channel_id=1, replica_groups=mesh['win'=128,'head'=4] {'win'}, dimensions={0} | all-to-all | bytes 1572864 | tf_op jit(solution)/shard_map/all_to_all | solution.py:193
  63.9 0.0 copy-start.1
  63.9 0.0 copy-done.3
  63.9 2.8 %shard_map.96 = bf16[1024,384]{1,0:T(8,128)(2,1)S(1)} custom-call(bf16[1024,384]{1,0:T(8,128)(2,1)S(1)} %bitcast.9, s32[64,128]{1,0:T(8,128)S(1)} %bitcast.13, s32[64,128]{1,0:T(8,128)S(1)} %bitcast.16), custom_call_target="tpu_custom_call" | custom-call | tf_op jit(solution)/shard_map/pallas_call | solution.py:224
  66.7 31.5 %all_to_all.21 = bf16[128,8,384]{2,1,0:T(8,128)(2,1)S(1)} all-to-all(bf16[128,8,384]{2,1,0:T(8,128)(2,1)S(1)} %bitcast.10), channel_id=1, replica_groups=mesh['win'=128,'head'=4] {'win'}, dimensions={0} | all-to-all | bytes 1572864 | tf_op jit(solution)/shard_map/all_to_all | solution.py:193
  98.2 0.0 copy-done.1
  98.2 2.9 %shard_map.98 = bf16[4,128,640]{2,1,0:T(8,128)(2,1)} custom-call(bf16[1024,384]{1,0:T(8,128)(2,1)S(1)} %bitcast.6, s32[64,128]{1,0:T(8,128)S(1)} %bitcast.14, bf16[2560,384]{1,0:T(8,128)(2,1)S(1)} %copy-done, bf16[2560,384]{1,0:T(8,128)(2,1)S(1)} %copy-done.1), custom_call_target="tpu_custom_call" | custom-call | tf_op jit(solution)/shard_map/pallas_call | solution.py:228
  101.1 3.5 %all-to-all-start.3 = ((bf16[4,128,640]{2,1,0:T(8,128)(2,1)}), bf16[4,128,640]{2,1,0:T(8,128)(2,1)S(1)}, u32[]{:S(2)}, u32[]{:S(2)}) async-start(bf16[4,128,640]{2,1,0:T(8,128)(2,1)} %shard_map.98), calls=%async_computation.3 | async-start | bytes 1310720 | tf_op jit(solution)/shard_map/all_to_all | solution.py:234
  104.5 1.3 %shard_map.97 = (bf16[128,384]{1,0:T(8,128)(2,1)}, bf16[128,384]{1,0:T(8,128)(2,1)}) custom-call(bf16[1024,384]{1,0:T(8,128)(2,1)S(1)} %bitcast.7, s32[64,128]{1,0:T(8,128)S(1)} %bitcast.15), custom_call_target="tpu_custom_call" | custom-call | tf_op jit(solution)/shard_map/pallas_call | solution.py:231
  105.9 8.5 %all-to-all-done.3 = bf16[4,128,640]{2,1,0:T(8,128)(2,1)S(1)} async-done(((bf16[4,128,640]{2,1,0:T(8,128)(2,1)}), bf16[4,128,640]{2,1,0:T(8,128)(2,1)S(1)}, u32[]{:S(2)}, u32[]{:S(2)}) %all-to-all-start.3) | async-done | bytes 655392 | tf_op jit(solution)/shard_map/all_to_all | solution.py:234
  114.4 0.8 reduce_sum.12
Async XLA Ops:
  0.6 17.1 %copy-start.2 = (s32[128,64]{0,1:T(8,128)S(1)}, s32[128,64]{0,1:T(8,128)}, u32[]{:S(2)}) copy-start(s32[128,64]{0,1:T(8,128)} %param.12) | copy-start | bytes 98308
  0.6 17.1 %copy-start = (bf16[2560,384]{1,0:T(8,128)(2,1)S(1)}, bf16[2560,384]{1,0:T(8,128)(2,1)}, u32[]{:S(2)}) copy-start(bf16[2560,384]{1,0:T(8,128)(2,1)} %refs_2_.3) | copy-start | bytes 5898244
  2.6 15.2 %all-to-all-start = ((bf16[4,128,640]{2,1,0:T(8,128)(2,1)}), bf16[4,128,640]{2,1,0:T(8,128)(2,1)S(1)}, u32[]{:S(2)}, u32[]{:S(2)}) async-start(bf16[4,128,640]{2,1,0:T(8,128)(2,1)} %broadcast_in_dim.2), calls=%async_computation | async-start | bytes 1310720 | tf_op jit(solution)/shard_map/all_to_all | solution.py:200
  8.3 55.6 %copy-start.3 = (s32[128,64]{0,1:T(8,128)S(1)}, s32[128,64]{0,1:T(8,128)}, u32[]{:S(2)}) copy-start(s32[128,64]{0,1:T(8,128)} %param.13) | copy-start | bytes 98308
  63.9 34.3 %copy-start.1 = (bf16[2560,384]{1,0:T(8,128)(2,1)S(1)}, bf16[2560,384]{1,0:T(8,128)(2,1)}, u32[]{:S(2)}) copy-start(bf16[2560,384]{1,0:T(8,128)(2,1)} %refs_3_.3) | copy-start | bytes 5898244
  101.1 13.3 %all-to-all-start.3 = ((bf16[4,128,640]{2,1,0:T(8,128)(2,1)}), bf16[4,128,640]{2,1,0:T(8,128)(2,1)S(1)}, u32[]{:S(2)}, u32[]{:S(2)}) async-start(bf16[4,128,640]{2,1,0:T(8,128)(2,1)} %shard_map.98), calls=%async_computation.3 | async-start | bytes 1310720 | tf_op jit(solution)/shard_map/all_to_all | solution.py:234
